TPU v7x, 32 devices: a whole 2x2x4 slice. The times are simulated.
32 devices in a mesh: design: 2 (over y), space: 8 (over z, x), case: 2 (over core).
Axes of the slice: x: 2, y: 2, z: 4, core: 2. Of those that a mesh axis runs over, the one named last changes fastest.
Arguments:
- displacement: float32 [16, 3, 96, 16, 128], P(('design', 'case'), None, 'space'), parts along dimension 0, may hold values from -3 to 3
- forces: float32 [16, 3, 96, 16, 128], P(('design', 'case'), None, 'space'), parts along dimension 0, may hold values from -13.6 to 13.6
- density: float32 [192, 16, 128], P(('design', 'space')), parts along dimension 0, may hold values from 0.1 to 1
- support_mask: int32 [192, 16, 128], P(('design', 'space')), parts along dimension 0, may hold values 0 or 1
- void_mask: int32 [192, 16, 128], P(('design', 'space')), parts along dimension 0, may hold values 0 or 1
Outputs:
- smoothed: float32 [16, 3, 96, 16, 128], P(('design', 'case'), None, 'space'), parts along dimension 0
- new_density: float32 [192, 16, 128], P(('design', 'space')), parts along dimension 0
- ks_value: float32 [2], P('design'), parts along dimension 0
There are 2 independent parts, one for each index of `design`. A program takes and returns all parts, laid end to end along the dimension named above; each array names one. Nothing has to cross between parts.
All inputs are finite; a program needn't handle non-finite values. No bound on the sum of `support_mask` or of `void_mask` on one device may be relied on, other than what follows from the above.
Results may differ from a plain program's by a relative error of at most 0.00002.
Values sent between devices are 32-bit elements; how exact they have to be, the bound alone decides.
A program may use at most 64 MiB of HBM per device.

v0:
```python
import math

import jax
import jax.numpy as jnp
from jax import lax
from jax.sharding import PartitionSpec as P

STIFF_MIN = 0.001
DIAG_SHIFT = 0.5
KS_BETA = 8.0
MOVE_LIMIT = 0.2
DENSITY_MIN = 0.001
STEP_ONE = 1.0 / (1.15 + 0.85 * math.cos(math.pi / 4))
STEP_TWO = 1.0 / (1.15 - 0.85 * math.cos(math.pi / 4))


def with_halo(block, sides, width):
    for axis, dim in sides:
        count = lax.axis_size(axis)
        forward = [(i, i + 1) for i in range(count - 1)]
        backward = [(target, source) for source, target in forward]
        low = lax.ppermute(
            lax.slice_in_dim(block, block.shape[dim] - width, None, axis=dim), axis, forward
        )
        high = lax.ppermute(lax.slice_in_dim(block, 0, width, axis=dim), axis, backward)
        block = jnp.concatenate([low, block, high], axis=dim)
    return block


def pad_axis(values, axis, width):
    widths = [(0, 0)] * values.ndim
    widths[values.ndim + axis] = (width, width)
    return jnp.pad(values, widths)


def stencil(fields, cube):
    face_x = STIFF_MIN + 0.5 * (cube[:-1] + cube[1:])
    middle = cube[1:-1]
    cube_y = pad_axis(middle, -2, 1)
    face_y = STIFF_MIN + 0.5 * (cube_y[:, :-1] + cube_y[:, 1:])
    cube_z = pad_axis(middle, -1, 1)
    face_z = STIFF_MIN + 0.5 * (cube_z[:, :, :-1] + cube_z[:, :, 1:])
    centre = fields[..., 1:-1, :, :]
    padded_y = pad_axis(centre, -2, 1)
    padded_z = pad_axis(centre, -1, 1)
    fluxes = face_x[1:] * (centre - fields[..., 2:, :, :]) + face_x[:-1] * (
        centre - fields[..., :-2, :, :]
    )
    fluxes = (
        fluxes
        + face_y[:, 1:] * (centre - padded_y[..., 2:, :])
        + face_y[:, :-1] * (centre - padded_y[..., :-2, :])
    )
    fluxes = (
        fluxes
        + face_z[:, :, 1:] * (centre - padded_z[..., 2:])
        + face_z[:, :, :-1] * (centre - padded_z[..., :-2])
    )
    diagonal = (
        DIAG_SHIFT
        + face_x[1:]
        + face_x[:-1]
        + face_y[:, 1:]
        + face_y[:, :-1]
        + face_z[:, :, 1:]
        + face_z[:, :, :-1]
    )
    return (DIAG_SHIFT * centre + fluxes, diagonal)


def smooth_sweep(fields, loads, cube, keep, factor):
    applied, diagonal = stencil(fields, cube)
    centre = fields[..., 1:-1, :, :]
    return keep * (centre + factor * (loads - applied) / diagonal)


def energy(extended, density):
    centre = extended[..., 1:-1, :, :]
    padded_y = pad_axis(centre, -2, 1)
    padded_z = pad_axis(centre, -1, 1)
    squares = (centre - extended[..., 2:, :, :]) ** 2 + (centre - extended[..., :-2, :, :]) ** 2
    squares = squares + (centre - padded_y[..., 2:, :]) ** 2 + (centre - padded_y[..., :-2, :]) ** 2
    squares = squares + (centre - padded_z[..., 2:]) ** 2 + (centre - padded_z[..., :-2]) ** 2
    return -1.5 * density * density * jnp.sum(squares, axis=-4)


def face_rim(motion):
    return with_halo(motion, (("space", 2),), 1)


def body(displacement, forces, density, support_mask, void_mask):
    planes = density.shape[0]
    rows_y = density.shape[1]
    rows_z = density.shape[2]
    slab_index = lax.axis_index("space")
    total_planes = planes * lax.axis_size("space")
    cells = total_planes * rows_y * rows_z
    keep = (1 - support_mask).astype(jnp.float32)
    cube_ext = with_halo(density, (("space", 0),), 1) ** 3
    motion = smooth_sweep(face_rim(displacement), forces, cube_ext, keep, STEP_ONE)
    motion = smooth_sweep(face_rim(motion), forces, cube_ext, keep, STEP_TWO)
    extended = face_rim(motion)
    case_sens = energy(extended, density)
    local_work = jnp.sum(forces * motion, axis=(1, 2, 3, 4))
    score_scale = KS_BETA / (3.0 * cells)
    scores = score_scale * lax.psum(local_work, "space")
    highest = lax.pmax(jnp.max(scores), "case")
    exponent = jnp.exp(scores - highest)
    denominator = lax.psum(jnp.sum(exponent), "case")
    weights = exponent / denominator
    ks_value = (highest + jnp.log(denominator)) / KS_BETA
    combined = lax.psum(jnp.sum(weights[:, None, None, None] * case_sens, axis=0), "case")
    product = density * combined
    rim_rows = with_halo(product, (("space", 0),), 1)
    padded_y = pad_axis(product, -2, 1)
    padded_z = pad_axis(product, -1, 1)
    neighbours = (
        rim_rows[2:]
        + rim_rows[:-2]
        + padded_y[:, 2:]
        + padded_y[:, :-2]
        + padded_z[:, :, 2:]
        + padded_z[:, :, :-2]
    )
    plane_ids = slab_index * planes + jnp.arange(planes)
    x_count = (plane_ids > 0).astype(jnp.float32) + (plane_ids < total_planes - 1).astype(
        jnp.float32
    )
    y_ids = jnp.arange(rows_y)
    y_count = (y_ids > 0).astype(jnp.float32) + (y_ids < rows_y - 1).astype(jnp.float32)
    z_ids = jnp.arange(rows_z)
    z_count = (z_ids > 0).astype(jnp.float32) + (z_ids < rows_z - 1).astype(jnp.float32)
    counts = x_count[:, None, None] + y_count[None, :, None] + z_count[None, None, :]
    filtered = (2.0 * product + neighbours) / (density * (2.0 + counts))
    scale = lax.psum(jnp.sum(-filtered), "space") / cells + 1e-06
    updated = jnp.clip(density + MOVE_LIMIT * (-filtered / scale - 1.0), DENSITY_MIN, 1.0)
    new_density = jnp.where(void_mask == 1, DENSITY_MIN, updated)
    return (motion, new_density, ks_value.reshape(1))


def solution(mesh):
    return jax.shard_map(
        body,
        mesh=mesh,
        in_specs=(
            P(("design", "case"), None, "space", None, None),
            P(("design", "case"), None, "space", None, None),
            P(("design", "space"), None, None),
            P(("design", "space"), None, None),
            P(("design", "space"), None, None),
        ),
        out_specs=(
            P(("design", "case"), None, "space", None, None),
            P(("design", "space"), None, None),
            P("design"),
        ),
        check_vma=False,
    )
```

profile of v0, /device:TPU:0, one launch (start us, length us, event | category | flops | bytes accessed | tf_op | source)
XLA Modules:
  0.0 140.1 jit_solution(4590353172492582459)
XLA Ops:
  7.2 0.0 all-reduce.12.cloned.1.call-start
  7.2 0.7 fusion.90
  7.9 4.9 %collective-permute-start = (f32[1,16,128]{2,1,0:T(8,128)S(1)}, f32[1,16,128]{2,1,0:T(8,128)S(1)}, u32[]{:S(2)}, u32[]{:S(2)}) collective-permute-start(f32[1,16,128]{2,1,0:T(8,128)S(1)} %get-tuple-element.25), channel_id=1, source_target_pairs={{0,2},{2,4},{4,6},{6,8},{8,10},{10,12},{12,14},{1,3},{3,5},{5,7},{... | collective-permute-start | bytes 24584 | tf_op jit(solution)/shard_map/ppermute | solution.py:22
  12.8 1.3 collective-permute-start.1
  14.1 1.0 fusion.87
  15.1 1.3 collective-permute-start.2
  16.4 5.2 %collective-permute-start.3 = (f32[4,3,1,16,128]{4,3,2,1,0:T(8,128)S(1)}, f32[4,3,1,16,128]{4,3,2,1,0:T(8,128)S(1)}, u32[]{:S(2)}, u32[]{:S(2)}) collective-permute-start(f32[4,3,1,16,128]{4,3,2,1,0:T(8,128)S(1)} %get-tuple-element.12), channel_id=1, source_target_pairs={{0,2},{2,4},{4,6},{6,8},{8,10},{10,12},{12,14},{1,3},{3,5},{5,7},{... | collective-permute-start | bytes 294920 | tf_op jit(solution)/shard_map/ppermute | solution.py:22
  21.5 0.9 subtract_convert_fusion
  22.5 0.0 collective-permute-done
  22.5 0.9 multiply_multiply_fusion.1
  23.4 0.0 collective-permute-done.1
  23.4 0.0 copy-start.3
  23.4 0.0 copy-start
  23.5 0.1 fusion.66
  23.7 0.1 fusion.88
  23.8 0.0 collective-permute-done.2
  23.8 0.3 collective-permute-done.3
  24.1 0.6 copy-done.3
  24.7 0.4 copy-done
  25.0 1.5 %fusion.63 = f32[4,3,12,16,128]{4,3,2,1,0:T(8,128)S(1)} fusion(f32[4,3,12,16,128]{4,3,2,1,0:T(8,128)S(1)} %copy-done.3, f32[4,3,12,16,128]{4,3,2,1,0:T(8,128)S(1)} %copy-done, f32[4,3,1,16,128]{4,3,2,1,0:T(8,128)S(1)} %collective-permute-done.3, f32[4,3,1,16,128]{4,3,2,1,0:T(8,128)S(1)} %collective-permute-done.2, f32[12,16,128]{2,1,0:T(8,128)S(1)} %get-tuple-element.14, ...), kind=kLoop, calls=%fused_computation.82 | loop fusion | flops 7667712 | bytes 4521984 | tf_op jit(solution)/shard_map/mul | solution.py:74
  26.5 1.3 collective-permute-start.4
  27.8 6.1 %collective-permute-start.5 = (f32[4,3,1,16,128]{4,3,2,1,0:T(8,128)S(1)}, f32[4,3,1,16,128]{4,3,2,1,0:T(8,128)}, u32[]{:S(2)}, u32[]{:S(2)}) collective-permute-start(f32[4,3,1,16,128]{4,3,2,1,0:T(8,128)S(1)} %get-tuple-element.10), channel_id=1, source_target_pairs={{0,2},{2,4},{4,6},{6,8},{8,10},{10,12},{12,14},{1,3},{3,5},{5,7},{... | collective-permute-start | bytes 294920 | tf_op jit(solution)/shard_map/ppermute | solution.py:22
  33.9 0.0 collective-permute-done.4
  34.0 1.5 %collective-permute-done.5 = f32[4,3,1,16,128]{4,3,2,1,0:T(8,128)} collective-permute-done((f32[4,3,1,16,128]{4,3,2,1,0:T(8,128)S(1)}, f32[4,3,1,16,128]{4,3,2,1,0:T(8,128)}, u32[]{:S(2)}, u32[]{:S(2)}) %collective-permute-start.5) | collective-permute-done | bytes 98336 | tf_op jit(solution)/shard_map/ppermute | solution.py:22
  35.5 2.4 %fusion.62 = f32[4,3,12,16,128]{4,3,2,1,0:T(8,128)S(1)} fusion(f32[4,3,12,16,128]{4,3,2,1,0:T(8,128)S(1)} %fusion.63, f32[4,3,12,16,128]{4,3,2,1,0:T(8,128)S(1)} %copy-done, f32[4,3,1,16,128]{4,3,2,1,0:T(8,128)} %collective-permute-done.5, f32[4,3,1,16,128]{4,3,2,1,0:T(8,128)S(1)} %collective-permute-done.4, f32[12,16,128]{2,1,0:T(8,128)S(1)} %get-tuple-element.14, ...), kind=kLoop, calls=%fused_computation.81 | loop fusion | flops 7667712 | bytes 4521984 | tf_op jit(solution)/shard_map/mul | solution.py:74
  37.9 0.0 copy-start.1
  37.9 1.3 collective-permute-start.6
  39.2 5.5 %collective-permute-start.7 = (f32[4,3,1,16,128]{4,3,2,1,0:T(8,128)S(1)}, f32[4,3,1,16,128]{4,3,2,1,0:T(8,128)S(1)}, u32[]{:S(2)}, u32[]{:S(2)}) collective-permute-start(f32[4,3,1,16,128]{4,3,2,1,0:T(8,128)S(1)} %get-tuple-element.8), channel_id=1, source_target_pairs={{0,2},{2,4},{4,6},{6,8},{8,10},{10,12},{12,14},{1,3},{3,5},{5,7},{... | collective-permute-start | bytes 294920 | tf_op jit(solution)/shard_map/ppermute | solution.py:22
  44.7 0.0 copy-start.2
  44.7 0.6 collective-permute-done.6
  45.3 2.0 %collective-permute-done.7 = f32[4,3,1,16,128]{4,3,2,1,0:T(8,128)S(1)} collective-permute-done((f32[4,3,1,16,128]{4,3,2,1,0:T(8,128)S(1)}, f32[4,3,1,16,128]{4,3,2,1,0:T(8,128)S(1)}, u32[]{:S(2)}, u32[]{:S(2)}) %collective-permute-start.7) | collective-permute-done | bytes 98336 | tf_op jit(solution)/shard_map/ppermute | solution.py:22
  47.3 1.1 multiply_reduce_fusion
  48.3 0.0 copy-done.1
  48.4 0.0 copy-start.4
  48.4 24.6 %psum.28 = f32[4]{0:T(128)S(1)} all-reduce(f32[4]{0:T(128)S(1)} %get-tuple-element.3), channel_id=1, replica_groups=mesh['design'=2,'space'=8,'case'=2] {'space'}, use_global_device_ids=true, to_apply=%region_1.2 | all-reduce | flops 4 | bytes 32 | tf_op jit(solution)/shard_map/psum | solution.py:106
  73.0 0.6 multiply_reduce_fusion.2
  73.6 3.1 %pmax.7 = f32[]{:T(128)} all-reduce(f32[]{:T(128)} %multiply_reduce_fusion.2), channel_id=1, replica_groups=mesh['design'=2,'space'=8,'case'=2] {'case'}, use_global_device_ids=true, to_apply=%region_3.4 | all-reduce | flops 1 | bytes 8 | tf_op jit(solution)/shard_map/pmax | solution.py:107
  76.7 1.3 fusion.82
  78.0 3.1 %psum.29 = f32[]{:T(128)} all-reduce(f32[]{:T(128)} %fusion.82), channel_id=1, replica_groups=mesh['design'=2,'space'=8,'case'=2] {'case'}, use_global_device_ids=true, to_apply=%region_5.6 | all-reduce | flops 1 | bytes 8 | tf_op jit(solution)/shard_map/psum | solution.py:109
  81.0 1.2 broadcast_divide_fusion
  82.2 0.7 multiply_reduce_fusion.1
  83.0 0.0 all-reduce.12.cloned.1.call-update
  83.0 0.1 broadcast_add_fusion
  83.1 15.2 %all-reduce.12.cloned.1.call-done = f32[12,16,128]{2,1,0:T(8,128)} async-done(((f32[12,16,128]{2,1,0:T(8,128)}), f32[12,16,128]{2,1,0:T(8,128)}) %all-reduce.12.cloned.1.call-update) | async-done | bytes 98320 | tf_op jit(solution)/shard_map/psum | solution.py:112
  98.3 0.0 copy-done.2
  98.3 0.9 mul.216
  99.2 1.3 collective-permute-start.8
  100.5 4.5 %collective-permute-start.9 = (f32[1,16,128]{2,1,0:T(8,128)S(1)}, f32[1,16,128]{2,1,0:T(8,128)S(1)}, u32[]{:S(2)}, u32[]{:S(2)}) collective-permute-start(f32[1,16,128]{2,1,0:T(8,128)S(1)} %get-tuple-element.21), channel_id=1, source_target_pairs={{0,2},{2,4},{4,6},{6,8},{8,10},{10,12},{12,14},{1,3},{3,5},{5,7},{... | collective-permute-start | bytes 24584 | tf_op jit(solution)/shard_map/ppermute | solution.py:22
  106.3 0.0 collective-permute-done.8
  106.3 0.1 collective-permute-done.9
  106.4 0.7 fusion.83
  107.8 23.0 %psum.31 = f32[]{:T(128)} all-reduce(f32[]{:T(128)S(6)} %neg.7), channel_id=1, replica_groups=mesh['design'=2,'space'=8,'case'=2] {'space'}, use_global_device_ids=true, to_apply=%region_10.11 | all-reduce | flops 1 | bytes 8 | tf_op jit(solution)/shard_map/psum | solution.py:135
  131.4 0.0 copy-done.4
  131.4 0.7 clamp_select_fusion
  (12 shorter events, 0.1 us)
Async XLA Ops:
  7.2 91.1 %all-reduce.12.cloned.1.call-start = ((), (), s32[]{:S(2)}) async-start(), calls=%async_computation | async-start | bytes 196608 | tf_op jit(solution)/shard_map/psum | solution.py:112
  7.9 14.5 %collective-permute-start = (f32[1,16,128]{2,1,0:T(8,128)S(1)}, f32[1,16,128]{2,1,0:T(8,128)S(1)}, u32[]{:S(2)}, u32[]{:S(2)}) collective-permute-start(f32[1,16,128]{2,1,0:T(8,128)S(1)} %get-tuple-element.25), channel_id=1, source_target_pairs={{0,2},{2,4},{4,6},{6,8},{8,10},{10,12},{12,14},{1,3},{3,5},{5,7},{... | collective-permute-start | bytes 24584 | tf_op jit(solution)/shard_map/ppermute | solution.py:22
  12.8 10.6 %collective-permute-start.1 = (f32[1,16,128]{2,1,0:T(8,128)S(1)}, f32[1,16,128]{2,1,0:T(8,128)S(1)}, u32[]{:S(2)}, u32[]{:S(2)}) collective-permute-start(f32[1,16,128]{2,1,0:T(8,128)S(1)} %get-tuple-element.24), channel_id=1, source_target_pairs={{2,0},{4,2},{6,4},{8,6},{10,8},{12,10},{14,12},{3,1},{5,3},{7,5},{... | collective-permute-start | bytes 24584 | tf_op jit(solution)/shard_map/ppermute | solution.py:25
  15.1 8.7 %collective-permute-start.2 = (f32[4,3,1,16,128]{4,3,2,1,0:T(8,128)S(1)}, f32[4,3,1,16,128]{4,3,2,1,0:T(8,128)S(1)}, u32[]{:S(2)}, u32[]{:S(2)}) collective-permute-start(f32[4,3,1,16,128]{4,3,2,1,0:T(8,128)S(1)} %get-tuple-element.11), channel_id=1, source_target_pairs={{2,0},{4,2},{6,4},{8,6},{10,8},{12,10},{14,12},{3,1},{5,3},{7,5},{... | collective-permute-start | bytes 294920 | tf_op jit(solution)/shard_map/ppermute | solution.py:25
  16.4 7.7 %collective-permute-start.3 = (f32[4,3,1,16,128]{4,3,2,1,0:T(8,128)S(1)}, f32[4,3,1,16,128]{4,3,2,1,0:T(8,128)S(1)}, u32[]{:S(2)}, u32[]{:S(2)}) collective-permute-start(f32[4,3,1,16,128]{4,3,2,1,0:T(8,128)S(1)} %get-tuple-element.12), channel_id=1, source_target_pairs={{0,2},{2,4},{4,6},{6,8},{8,10},{10,12},{12,14},{1,3},{3,5},{5,7},{... | collective-permute-start | bytes 294920 | tf_op jit(solution)/shard_map/ppermute | solution.py:22
  23.4 1.3 copy-start.3
  23.4 1.6 %copy-start = (f32[4,3,12,16,128]{4,3,2,1,0:T(8,128)S(1)}, f32[4,3,12,16,128]{4,3,2,1,0:T(8,128)}, u32[]{:S(2)}) copy-start(f32[4,3,12,16,128]{4,3,2,1,0:T(8,128)} %param.6) | copy-start | bytes 3538948
  26.5 7.4 %collective-permute-start.4 = (f32[4,3,1,16,128]{4,3,2,1,0:T(8,128)S(1)}, f32[4,3,1,16,128]{4,3,2,1,0:T(8,128)S(1)}, u32[]{:S(2)}, u32[]{:S(2)}) collective-permute-start(f32[4,3,1,16,128]{4,3,2,1,0:T(8,128)S(1)} %get-tuple-element.9), channel_id=1, source_target_pairs={{2,0},{4,2},{6,4},{8,6},{10,8},{12,10},{14,12},{3,1},{5,3},{7,5},{... | collective-permute-start | bytes 294920 | tf_op jit(solution)/shard_map/ppermute | solution.py:25
  27.8 7.6 %collective-permute-start.5 = (f32[4,3,1,16,128]{4,3,2,1,0:T(8,128)S(1)}, f32[4,3,1,16,128]{4,3,2,1,0:T(8,128)}, u32[]{:S(2)}, u32[]{:S(2)}) collective-permute-start(f32[4,3,1,16,128]{4,3,2,1,0:T(8,128)S(1)} %get-tuple-element.10), channel_id=1, source_target_pairs={{0,2},{2,4},{4,6},{6,8},{8,10},{10,12},{12,14},{1,3},{3,5},{5,7},{... | collective-permute-start | bytes 294920 | tf_op jit(solution)/shard_map/ppermute | solution.py:22
  37.9 10.5 %copy-start.1 = (f32[4,3,12,16,128]{4,3,2,1,0:T(8,128)}, f32[4,3,12,16,128]{4,3,2,1,0:T(8,128)S(1)}, u32[]{:S(2)}) copy-start(f32[4,3,12,16,128]{4,3,2,1,0:T(8,128)S(1)} %fusion.62) | copy-start | bytes 3538948
  37.9 7.4 %collective-permute-start.6 = (f32[4,3,1,16,128]{4,3,2,1,0:T(8,128)S(1)}, f32[4,3,1,16,128]{4,3,2,1,0:T(8,128)S(1)}, u32[]{:S(2)}, u32[]{:S(2)}) collective-permute-start(f32[4,3,1,16,128]{4,3,2,1,0:T(8,128)S(1)} %get-tuple-element.7), channel_id=1, source_target_pairs={{2,0},{4,2},{6,4},{8,6},{10,8},{12,10},{14,12},{3,1},{5,3},{7,5},{... | collective-permute-start | bytes 294920 | tf_op jit(solution)/shard_map/ppermute | solution.py:25
  39.2 8.1 %collective-permute-start.7 = (f32[4,3,1,16,128]{4,3,2,1,0:T(8,128)S(1)}, f32[4,3,1,16,128]{4,3,2,1,0:T(8,128)S(1)}, u32[]{:S(2)}, u32[]{:S(2)}) collective-permute-start(f32[4,3,1,16,128]{4,3,2,1,0:T(8,128)S(1)} %get-tuple-element.8), channel_id=1, source_target_pairs={{0,2},{2,4},{4,6},{6,8},{8,10},{10,12},{12,14},{1,3},{3,5},{5,7},{... | collective-permute-start | bytes 294920 | tf_op jit(solution)/shard_map/ppermute | solution.py:22
  44.7 53.6 %copy-start.2 = (f32[12,16,128]{2,1,0:T(8,128)S(1)}, f32[12,16,128]{2,1,0:T(8,128)}, u32[]{:S(2)}) copy-start(f32[12,16,128]{2,1,0:T(8,128)} %param.7) | copy-start | bytes 294916
  48.4 83.1 %copy-start.4 = (s32[12,16,128]{2,1,0:T(8,128)S(1)}, s32[12,16,128]{2,1,0:T(8,128)}, u32[]{:S(2)}) copy-start(s32[12,16,128]{2,1,0:T(8,128)} %param.9) | copy-start | bytes 294916
  99.2 7.1 %collective-permute-start.8 = (f32[1,16,128]{2,1,0:T(8,128)S(1)}, f32[1,16,128]{2,1,0:T(8,128)S(1)}, u32[]{:S(2)}, u32[]{:S(2)}) collective-permute-start(f32[1,16,128]{2,1,0:T(8,128)S(1)} %get-tuple-element.20), channel_id=1, source_target_pairs={{2,0},{4,2},{6,4},{8,6},{10,8},{12,10},{14,12},{3,1},{5,3},{7,5},{... | collective-permute-start | bytes 24584 | tf_op jit(solution)/shard_map/ppermute | solution.py:25
  100.5 5.9 %collective-permute-start.9 = (f32[1,16,128]{2,1,0:T(8,128)S(1)}, f32[1,16,128]{2,1,0:T(8,128)S(1)}, u32[]{:S(2)}, u32[]{:S(2)}) collective-permute-start(f32[1,16,128]{2,1,0:T(8,128)S(1)} %get-tuple-element.21), channel_id=1, source_target_pairs={{0,2},{2,4},{4,6},{6,8},{8,10},{10,12},{12,14},{1,3},{3,5},{5,7},{... | collective-permute-start | bytes 24584 | tf_op jit(solution)/shard_map/ppermute | solution.py:22
Sparse Core Ops, SparseCore 0:
  83.1 15.0 all-reduce.11
where the time goes:
time: 141 us; the launch traced here: 140 us
  blocking collectives  53.8 us (38%)
  starting transfers between devices  32.6 us (23%)
  waiting for transfers between devices  19.8 us (14%)
  between operations  18 us (13%)
  other arithmetic  13.2 us (9%)
  local copies, waits for them, and re-layouts  2.71 us (2%)
    ppermute x5, starting transfers between devices, with_halo(): lax.ppermute(lax.slice_in_dim(block, block.shape[dim] - width, None, axis...  26.1 us
    psum x1, blocking collectives, body(): scores = score_scale * lax.psum(local_work, 'space')  24.6 us
    psum x1, blocking collectives, body(): scale = lax.psum(jnp.sum(-filtered), 'space') / cells + 1e-06  23 us
    psum x1, waiting for transfers between devices, body(): lax.psum(jnp.sum(weights[:, None, None, None] * case_sens, axis=0), 'case')  15.2 us
    ppermute x5, starting transfers between devices, with_halo(): lax.ppermute(lax.slice_in_dim(block, 0, width, axis=dim), axis, backward)  6.46 us
    ppermute x5, waiting for transfers between devices, with_halo(): lax.ppermute(lax.slice_in_dim(block, block.shape[dim] - width, None, axis...  3.92 us
    mul x2, other arithmetic, smooth_sweep(): return keep * (centre + factor * (loads - applied) / diagonal)  3.82 us
    pmax x1, blocking collectives, body(): highest = lax.pmax(jnp.max(scores), 'case')  3.08 us
  transfers between devices with their start and end apart: 11, of which 6 were waited for; matrix products, arithmetic and copies ran while one was open for 2% of the time, Pallas kernels for 0%

commit v1 on v0

v1 whole, which is shorter than its diff:
```python
import functools
import math

import jax
import jax.numpy as jnp
from jax import lax
from jax.experimental import pallas as pl
from jax.experimental.pallas import tpu as pltpu
from jax.sharding import PartitionSpec as P

STIFF_MIN = 0.001
DIAG_SHIFT = 0.5
KS_BETA = 8.0
MOVE_LIMIT = 0.2
DENSITY_MIN = 0.001
STEP_ONE = 1.0 / (1.15 + 0.85 * math.cos(math.pi / 4))
STEP_TWO = 1.0 / (1.15 - 0.85 * math.cos(math.pi / 4))
F32 = jnp.float32
MESH = pl.DeviceIdType.MESH


def kernel(
    n_space, n_case,
    disp, forces, dens, sup, void,
    out, newd, ks,
    v, f, s1, s2, d, cube, inv, sup_v, void_v,
    kx, kyp, kym, kzp, kzm, keep, rdk, hsum, e, u, up,
    acc, gath,
    load_sem, dens_load, out_sem,
    send_sem, recv_sem, dsend, drecv, usend, urecv, gsend, grecv,
):
    cases, comps, planes, rows, lanes = disp.shape
    s = lax.axis_index("space")
    mine = lax.axis_index("case")
    members = n_space * n_case
    me = s * n_case + mine
    has_lo = s > 0
    has_hi = s < n_space - 1
    lo = jnp.maximum(s - 1, 0)
    hi = jnp.minimum(s + 1, n_space - 1)
    last = planes + 1

    barrier = pltpu.get_barrier_semaphore()

    def greet(step, carry):
        peer = lax.rem(me + step, members)
        pl.semaphore_signal(
            barrier, inc=1,
            device_id={"space": peer // n_case, "case": lax.rem(peer, n_case)},
            device_id_type=MESH,
        )
        return carry

    lax.fori_loop(1, members, greet, 0)

    own = pl.ds(1, planes)
    dens_loads = [
        pltpu.make_async_copy(dens, d.at[own], dens_load.at[0]),
        pltpu.make_async_copy(sup, sup_v, dens_load.at[1]),
        pltpu.make_async_copy(void, void_v, dens_load.at[2]),
    ]
    for copy in dens_loads:
        copy.start()

    def disp_load(c):
        return pltpu.make_async_copy(disp.at[c], v.at[c, :, own], load_sem.at[0, c])

    def force_load(c):
        return pltpu.make_async_copy(forces.at[c], f.at[c], load_sem.at[1, c])

    for c in range(cases):
        disp_load(c).start()
        force_load(c).start()

    @pl.when(s == 0)
    def _():
        zero = jnp.zeros((rows, lanes), F32)
        d[0] = zero
        u[0] = zero
        up[0] = zero
        for ref in (v, s1, s2):
            ref[:, :, 0] = jnp.zeros((cases, comps, rows, lanes), F32)

    @pl.when(s == n_space - 1)
    def _():
        zero = jnp.zeros((rows, lanes), F32)
        d[last] = zero
        u[last] = zero
        up[last] = zero
        for ref in (v, s1, s2):
            ref[:, :, last] = jnp.zeros((cases, comps, rows, lanes), F32)

    pl.semaphore_wait(barrier, members - 1)

    def remote(src, dst, ssem, rsem, peer):
        return pltpu.make_async_remote_copy(
            src_ref=src, dst_ref=dst, send_sem=ssem, recv_sem=rsem,
            device_id={"space": peer}, device_id_type=MESH,
        )

    def dens_up():
        return remote(dens.at[planes - 1], d.at[0], dsend.at[0], drecv.at[0], hi)

    def dens_down():
        return remote(dens.at[0], d.at[last], dsend.at[1], drecv.at[1], lo)

    bufs = (v, s1, s2)

    def face_up(stage, c):
        src = disp.at[c, :, planes - 1] if stage == 0 else bufs[stage].at[c, :, planes]
        return remote(
            src, bufs[stage].at[c, :, 0], send_sem.at[stage, c, 0], recv_sem.at[stage, c, 0], hi
        )

    def face_down(stage, c):
        src = disp.at[c, :, 0] if stage == 0 else bufs[stage].at[c, :, 1]
        return remote(
            src, bufs[stage].at[c, :, last], send_sem.at[stage, c, 1], recv_sem.at[stage, c, 1], lo
        )

    def send_faces(stage, c):
        @pl.when(has_hi)
        def _():
            face_up(stage, c).start()

        @pl.when(has_lo)
        def _():
            face_down(stage, c).start()

    def await_faces(stage, c):
        @pl.when(has_lo)
        def _():
            face_up(stage, c).wait_recv()

        @pl.when(has_hi)
        def _():
            face_down(stage, c).wait_recv()

    @pl.when(has_hi)
    def _():
        dens_up().start()

    @pl.when(has_lo)
    def _():
        dens_down().start()

    for c in range(cases):
        send_faces(0, c)

    y_id = lax.broadcasted_iota(jnp.int32, (rows, lanes), 0)
    z_id = lax.broadcasted_iota(jnp.int32, (rows, lanes), 1)
    y_first, y_last = y_id == 0, y_id == rows - 1
    z_first, z_last = z_id == 0, z_id == lanes - 1
    yz_count = (
        4.0 + 2.0 - y_first.astype(F32) - y_last.astype(F32)
        - z_first.astype(F32) - z_last.astype(F32)
    )

    def next_y(value):
        return pltpu.roll(value, rows - 1, value.ndim - 2)

    def prev_y(value):
        return pltpu.roll(value, 1, value.ndim - 2)

    def next_z(value):
        return pltpu.roll(value, lanes - 1, value.ndim - 1)

    def prev_z(value):
        return pltpu.roll(value, 1, value.ndim - 1)

    def cube_of(j):
        value = d[j]
        cube[j] = value * value * value

    total_planes = planes * n_space

    def inv_of(j):
        g = s * planes + j - 1
        x_count = (g > 0).astype(F32) + (g < total_planes - 1).astype(F32)
        inside = jnp.logical_and(g >= 0, g < total_planes).astype(F32)
        value = jnp.where(d[j] > 0, d[j], 1.0)
        inv[j] = inside / (value * (yz_count + x_count))

    def coefficients(j):
        here = cube[j]
        face_lo = STIFF_MIN + 0.5 * (cube[j - 1] + here)
        face_hi = STIFF_MIN + 0.5 * (here + cube[j + 1])
        kx[j - 1] = face_lo
        kx[j] = face_hi
        y_hi = STIFF_MIN + 0.5 * (here + jnp.where(y_last, 0.0, next_y(here)))
        y_lo = STIFF_MIN + 0.5 * (here + jnp.where(y_first, 0.0, prev_y(here)))
        z_hi = STIFF_MIN + 0.5 * (here + jnp.where(z_last, 0.0, next_z(here)))
        z_lo = STIFF_MIN + 0.5 * (here + jnp.where(z_first, 0.0, prev_z(here)))
        diagonal = DIAG_SHIFT + face_hi + face_lo + y_hi + y_lo + z_hi + z_lo
        kyp[j - 1] = jnp.where(y_last, 0.0, y_hi)
        kym[j - 1] = jnp.where(y_first, 0.0, y_lo)
        kzp[j - 1] = jnp.where(z_last, 0.0, z_hi)
        kzm[j - 1] = jnp.where(z_first, 0.0, z_lo)
        kept = (1 - sup_v[j - 1]).astype(F32)
        keep[j - 1] = kept
        rdk[j - 1] = kept / diagonal

    def around(value):
        return (
            jnp.where(y_last, 0.0, next_y(value)) + jnp.where(y_first, 0.0, prev_y(value))
            + jnp.where(z_last, 0.0, next_z(value)) + jnp.where(z_first, 0.0, prev_z(value))
        )

    def filter_sum(j):
        here = inv[j]
        total = 2.0 * here + inv[j - 1] + inv[j + 1] + around(here)
        hsum[j - 1] = 1.5 * cube[j] * total

    def loop(start, stop, fn, unroll=1):
        def step(i, carry):
            fn(i)
            return carry

        lax.fori_loop(start, stop, step, 0, unroll=unroll)

    for copy in dens_loads:
        copy.wait()
    loop(1, last, cube_of)
    loop(1, last, inv_of)
    loop(2, planes, coefficients)

    def sweep(src, dst, c, j, factor):
        centre = src[c, :, j]
        load = f[c, :, j - 1]
        total = load + kx[j - 1] * src[c, :, j - 1] + kx[j] * src[c, :, j + 1]
        total = total + kyp[j - 1] * next_y(centre) + kym[j - 1] * prev_y(centre)
        total = total + kzp[j - 1] * next_z(centre) + kzm[j - 1] * prev_z(centre)
        result = (keep[j - 1] * (1.0 - factor)) * centre + (rdk[j - 1] * factor) * total
        dst[c, :, j] = result
        return load, result

    def energy(c, j):
        centre = s2[c, :, j]
        low = centre - s2[c, :, j - 1]
        high = centre - s2[c, :, j + 1]
        y_hi = centre - jnp.where(y_last, 0.0, next_y(centre))
        y_lo = centre - jnp.where(y_first, 0.0, prev_y(centre))
        z_hi = centre - jnp.where(z_last, 0.0, next_z(centre))
        z_lo = centre - jnp.where(z_first, 0.0, prev_z(centre))
        squares = low * low + high * high + y_hi * y_hi + y_lo * y_lo + z_hi * z_hi + z_lo * z_lo
        value = jnp.sum(squares, axis=0)
        e[c, j - 1] = value
        return value * hsum[j - 1]

    def interior_one(c):
        disp_load(c).wait()
        force_load(c).wait()
        loop(2, planes, lambda j: sweep(v, s1, c, j, STEP_ONE), unroll=2)

    loop(0, cases, interior_one)

    @pl.when(has_lo)
    def _():
        dens_up().wait_recv()

    @pl.when(has_hi)
    def _():
        dens_down().wait_recv()

    cube_of(0)
    cube_of(last)
    inv_of(0)
    inv_of(last)
    coefficients(1)
    coefficients(planes)
    loop(1, last, filter_sum)

    zero = jnp.zeros((rows, lanes), F32)

    def stage_one(c):
        await_faces(0, c)
        sweep(v, s1, c, 1, STEP_ONE)
        sweep(v, s1, c, planes, STEP_ONE)
        send_faces(1, c)

        def step(j, total):
            load, result = sweep(s1, s2, c, j, STEP_TWO)
            return total + jnp.sum(load * result, axis=0)

        acc[0, c] = lax.fori_loop(2, planes, step, zero, unroll=2)

    loop(0, cases, stage_one)

    def out_copy(c):
        return pltpu.make_async_copy(s2.at[c, :, own], out.at[c], out_sem.at[c])

    def stage_two(c):
        await_faces(1, c)
        load, result = sweep(s1, s2, c, 1, STEP_TWO)
        total = acc[0, c] + jnp.sum(load * result, axis=0)
        load, result = sweep(s1, s2, c, planes, STEP_TWO)
        acc[0, c] = total + jnp.sum(load * result, axis=0)
        send_faces(2, c)
        out_copy(c).start()
        acc[1, c] = lax.fori_loop(
            2, planes, lambda j, total: total + energy(c, j), zero, unroll=2
        )

    loop(0, cases, stage_two)

    lane = lax.broadcasted_iota(jnp.int32, (1, lanes), 1)

    def gather_copy(which, peer):
        return pltpu.make_async_remote_copy(
            src_ref=gath.at[which, me], dst_ref=gath.at[which, me],
            send_sem=gsend.at[which], recv_sem=grecv.at[which],
            device_id={"space": peer // n_case, "case": lax.rem(peer, n_case)},
            device_id_type=MESH,
        )

    def gather_start(which):
        row = jnp.zeros((1, lanes), F32)
        for c in range(cases):
            part = jnp.sum(jnp.sum(acc[which, c], axis=0, keepdims=True), axis=1, keepdims=True)
            row = jnp.where(lane == mine * cases + c, part, row)
        gath[which, me] = row
        loop(1, members, lambda step: gather_copy(which, lax.rem(me + step, members)).start())

    def whole(which):
        return gath.at[which, pl.ds(0, members - 1)]

    def gather_wait(which):
        pltpu.make_async_copy(whole(which), whole(which), grecv.at[which]).wait()
        return jnp.sum(gath[which], axis=0)

    gather_start(0)

    def stage_three(c):
        await_faces(2, c)
        acc[1, c] = acc[1, c] + energy(c, 1) + energy(c, planes)

    loop(0, cases, stage_three)
    gather_start(1)

    cells = total_planes * rows * lanes
    valid = lane < cases * n_case
    scores = (KS_BETA / (3.0 * cells)) * gather_wait(0)
    top = jnp.max(jnp.where(valid, scores, -3.0e38), axis=1, keepdims=True)
    exponent = jnp.where(valid, jnp.exp(jnp.where(valid, scores - top, 0.0)), 0.0)
    total = jnp.sum(exponent, axis=1, keepdims=True)
    weights = exponent / total
    ks[0] = jnp.max((top + jnp.log(total)) / KS_BETA)
    picks = [
        jnp.sum(jnp.where(lane == mine * cases + c, weights, 0.0), axis=1, keepdims=True)
        for c in range(cases)
    ]

    def mix(j):
        value = picks[0] * e[0, j - 1]
        for c in range(1, cases):
            value = value + picks[c] * e[c, j - 1]
        u[j] = value

    mix(1)
    mix(planes)

    other = 1 - mine if n_case == 2 else lax.rem(mine + 1, n_case)

    def rim(dst, index, peer, case, src):
        return pltpu.make_async_remote_copy(
            src_ref=u.at[src], dst_ref=dst,
            send_sem=usend.at[index], recv_sem=urecv.at[index],
            device_id={"space": peer, "case": case}, device_id_type=MESH,
        )

    rims_up = [rim(u.at[0], 0, hi, mine, planes), rim(up.at[0], 1, hi, other, planes)]
    rims_down = [rim(u.at[last], 2, lo, mine, 1), rim(up.at[last], 3, lo, other, 1)]

    @pl.when(has_hi)
    def _():
        for copy in rims_up:
            copy.start()

    @pl.when(has_lo)
    def _():
        for copy in rims_down:
            copy.start()

    loop(2, planes, mix, unroll=2)
    across = rim(up.at[own], 4, s, other, own)
    across.start()
    across.wait_recv()

    @pl.when(has_lo)
    def _():
        for copy in rims_up:
            copy.wait_recv()

    @pl.when(has_hi)
    def _():
        for copy in rims_down:
            copy.wait_recv()

    def product(j):
        cube[j] = 1.5 * cube[j] * (u[j] + up[j])

    loop(0, last + 1, product, unroll=2)

    def filtered(j):
        here = cube[j]
        kx[j - 1] = inv[j] * (2.0 * here + cube[j - 1] + cube[j + 1] + around(here))

    loop(1, last, filtered, unroll=2)

    sums = gather_wait(1)
    scale = jnp.sum(weights * jnp.where(valid, sums, 0.0), axis=1, keepdims=True) / cells + 1e-06

    def update(j):
        value = d[j] + MOVE_LIMIT * (kx[j - 1] / scale - 1.0)
        value = jnp.minimum(jnp.maximum(value, DENSITY_MIN), 1.0)
        newd[j - 1] = jnp.where(void_v[j - 1] == 1, DENSITY_MIN, value)

    loop(1, last, update, unroll=2)

    @pl.when(has_hi)
    def _():
        dens_up().wait_send()
        for copy in rims_up:
            copy.wait_send()
        for stage in range(3):
            loop(0, cases, lambda c: face_up(stage, c).wait_send())

    @pl.when(has_lo)
    def _():
        dens_down().wait_send()
        for copy in rims_down:
            copy.wait_send()
        for stage in range(3):
            loop(0, cases, lambda c: face_down(stage, c).wait_send())

    across.wait_send()
    for which in range(2):
        pltpu.make_async_copy(whole(which), whole(which), gsend.at[which]).wait()
    loop(0, cases, lambda c: out_copy(c).wait())


def solution(mesh):
    n_space, n_case = mesh.shape["space"], mesh.shape["case"]
    members = n_space * n_case

    def body(displacement, forces, density, support_mask, void_mask):
        cases, comps, planes, rows, lanes = displacement.shape
        padded = (cases, comps, planes + 2, rows, lanes)
        slab = (planes, rows, lanes)
        thick = (planes + 2, rows, lanes)
        any_space = pl.BlockSpec(memory_space=pl.ANY)
        vmem = lambda shape, dtype=F32: pltpu.VMEM(shape, dtype)
        dma = pltpu.SemaphoreType.DMA
        return pl.pallas_call(
            functools.partial(kernel, n_space, n_case),
            out_shape=(
                jax.ShapeDtypeStruct(displacement.shape, F32),
                jax.ShapeDtypeStruct(density.shape, F32),
                jax.ShapeDtypeStruct((1,), F32),
            ),
            in_specs=[any_space] * 5,
            out_specs=(
                any_space,
                pl.BlockSpec(memory_space=pltpu.VMEM),
                pl.BlockSpec(memory_space=pltpu.SMEM),
            ),
            scratch_shapes=[
                vmem(padded), vmem(displacement.shape), vmem(padded), vmem(padded),
                vmem(thick), vmem(thick), vmem(thick),
                vmem(slab, jnp.int32), vmem(slab, jnp.int32),
                vmem((planes + 1, rows, lanes)),
                vmem(slab), vmem(slab), vmem(slab), vmem(slab), vmem(slab), vmem(slab),
                vmem(slab),
                vmem((cases,) + slab), vmem(thick), vmem(thick),
                vmem((2, cases, rows, lanes)),
                vmem((2, members, 1, lanes)),
                dma((2, cases)), dma((3,)), dma((cases,)),
                dma((3, cases, 2)), dma((3, cases, 2)), dma((2,)), dma((2,)),
                dma((5,)), dma((5,)), dma((2,)), dma((2,)),
            ],
            compiler_params=pltpu.CompilerParams(collective_id=0, has_side_effects=True),
        )(displacement, forces, density, support_mask, void_mask)

    return jax.shard_map(
        body,
        mesh=mesh,
        in_specs=(
            P(("design", "case"), None, "space", None, None),
            P(("design", "case"), None, "space", None, None),
            P(("design", "space"), None, None),
            P(("design", "space"), None, None),
            P(("design", "space"), None, None),
        ),
        out_specs=(
            P(("design", "case"), None, "space", None, None),
            P(("design", "space"), None, None),
            P("design"),
        ),
        check_vma=False,
    )
```

time: 141 us -> 34.2 us (0.24)
  blocking collectives: 53.8 us -> 0 us
  starting transfers between devices: 32.6 us -> 0 us
  Pallas kernels: 0 us -> 28.5 us
  waiting for transfers between devices: 19.8 us -> 0 us
  between operations: 18 us -> 2.41 us
  other arithmetic: 13.2 us -> 0 us
    psum x3 -> x0, blocking collectives: 50.7 us -> none  [the longest x1 24.6 us: body(): scores = score_scale * lax.psum(local_work, 'space')]
    ppermute x10 -> x0, starting transfers between devices: 32.6 us -> none  [the longest x5 26.1 us: with_halo(): lax.ppermute(lax.slice_in_dim(block, block.shape[dim] - width, None, axis...]
    pallas_call x0 -> x1, Pallas kernels: none -> 28.5 us  [body(): pl.pallas_call(functools.partial(kernel, n_space, n_case), out_shape=(jax...]
    psum x1 -> x0, waiting for transfers between devices: 15.2 us -> none  [body(): lax.psum(jnp.sum(weights[:, None, None, None] * case_sens, axis=0), 'case')]
    mul x4 -> x0, other arithmetic: 5.64 us -> none  [the longest x2 3.82 us: smooth_sweep(): return keep * (centre + factor * (loads - applied) / diagonal)]
    ppermute x10 -> x0, waiting for transfers between devices: 4.59 us -> none  [the longest x5 3.92 us: with_halo(): lax.ppermute(lax.slice_in_dim(block, block.shape[dim] - width, None, axis...]
    reduce_sum x4 -> x0, other arithmetic: 3.79 us -> none  [the longest x1 1.25 us: body(): denominator = lax.psum(jnp.sum(exponent), 'case')]
    pmax x1 -> x0, blocking collectives: 3.08 us -> none  [body(): highest = lax.pmax(jnp.max(scores), 'case')]
  transfers between devices with their start and end apart: 11 -> 0, of which waited for: 6 -> 0; matrix products, arithmetic and copies ran while one was open for 2% -> 0% of each run, Pallas kernels for 0% -> 0%
where the time goes in v1:
time: 34.2 us; the launch traced here: 34 us
  Pallas kernels  28.5 us (83%)
  local copies, waits for them, and re-layouts  3.04 us (9%)
  between operations  2.41 us (7%)
    pallas_call x1, Pallas kernels, body(): pl.pallas_call(functools.partial(kernel, n_space, n_case), out_shape=(jax...  28.5 us
    unnamed x4, local copies, waits for them, and re-layouts  3.04 us

profile of v1, /device:TPU:0, one launch (start us, length us, event | category | flops | bytes accessed | tf_op | source)
XLA Modules:
  0.0 34.0 jit_solution(3671975761152427492)
XLA Ops:
  0.6 28.5 %shard_map.76 = (f32[4,3,12,16,128]{4,3,2,1,0:T(8,128)}, f32[12,16,128]{2,1,0:T(8,128)}, f32[1]{0:T(128)}) custom-call(f32[4,3,12,16,128]{4,3,2,1,0:T(8,128)} %disp.1, f32[4,3,12,16,128]{4,3,2,1,0:T(8,128)} %forces.1, f32[12,16,128]{2,1,0:T(8,128)} %dens.1, s32[12,16,128]{2,1,0:T(8,128)} %sup.1, s32[12,16,128]{2,1,0:T(8,128)} %void.1), custom_call_target="tpu_custom_call" | custom-call | tf_op jit(solution)/shard_map/pallas_call | solution.py:454
  29.2 0.0 copy-start
  29.2 2.4 %copy.11 = f32[4,3,12,16,128]{4,3,2,1,0:T(8,128)} copy(f32[4,3,12,16,128]{4,3,2,1,0:T(8,128)} %get-tuple-element.6) | data formatting | bytes 2359296
  31.6 0.0 copy-done
  31.6 0.6 %copy.12 = f32[12,16,128]{2,1,0:T(8,128)} copy(f32[12,16,128]{2,1,0:T(8,128)S(1)} %copy-done) | data formatting | bytes 196608
Async XLA Ops:
  29.2 2.4 %copy-start = (f32[12,16,128]{2,1,0:T(8,128)S(1)}, f32[12,16,128]{2,1,0:T(8,128)}, u32[]{:S(2)}) copy-start(f32[12,16,128]{2,1,0:T(8,128)} %get-tuple-element.7) | copy-start | bytes 294916

commit v2 on v1

--- a/solution.py
+++ b/solution.py
@@ -27,7 +27,7 @@
     kx, kyp, kym, kzp, kzm, keep, rdk, hsum, e, u, up,
     acc, gath,
     load_sem, dens_load, out_sem,
-    send_sem, recv_sem, dsend, drecv, usend, urecv, gsend, grecv,
+    send_sem, recv_sem, dsend, drecv, usend, urecv, gsend, grecv, known,
 ):
     cases, comps, planes, rows, lanes = disp.shape
     s = lax.axis_index("space")
@@ -40,18 +40,46 @@
     hi = jnp.minimum(s + 1, n_space - 1)
     last = planes + 1
 
+    other = 1 - mine if n_case == 2 else lax.rem(mine + 1, n_case)
+
     barrier = pltpu.get_barrier_semaphore()
 
-    def greet(step, carry):
-        peer = lax.rem(me + step, members)
+    def greet(sem, distance):
+        @pl.when(s >= distance)
+        def _():
+            pl.semaphore_signal(
+                sem, inc=1, device_id={"space": jnp.maximum(s - distance, 0)}, device_id_type=MESH
+            )
+
+        @pl.when(s < n_space - distance)
+        def _():
+            pl.semaphore_signal(
+                sem, inc=1, device_id={"space": jnp.minimum(s + distance, n_space - 1)},
+                device_id_type=MESH,
+            )
+
+    def greeted(distance):
+        return (s >= distance).astype(jnp.int32) + (s < n_space - distance).astype(jnp.int32)
+
+    greet(barrier, 1)
+    for step in range(1, n_case):
         pl.semaphore_signal(
-            barrier, inc=1,
-            device_id={"space": peer // n_case, "case": lax.rem(peer, n_case)},
-            device_id_type=MESH,
-        )
-        return carry
-
-    lax.fori_loop(1, members, greet, 0)
+            barrier, inc=1, device_id={"case": lax.rem(mine + step, n_case)}, device_id_type=MESH
+        )
+
+    distances = [1]
+    while distances[-1] < n_space:
+        distances.append(2 * distances[-1])
+    distances = [1] + distances[:-1] if n_space > 1 else []
+    distances = distances[1:]
+
+    def widen_start(k):
+        if k < len(distances):
+            greet(known.at[k], distances[k])
+
+    def widen_wait(k):
+        if k < len(distances):
+            pl.semaphore_wait(known.at[k], greeted(distances[k]))
 
     own = pl.ds(1, planes)
     dens_loads = [
@@ -90,7 +118,7 @@
         for ref in (v, s1, s2):
             ref[:, :, last] = jnp.zeros((cases, comps, rows, lanes), F32)
 
-    pl.semaphore_wait(barrier, members - 1)
+    pl.semaphore_wait(barrier, greeted(1) + (n_case - 1))
 
     def remote(src, dst, ssem, rsem, peer):
         return pltpu.make_async_remote_copy(
@@ -146,6 +174,7 @@
 
     for c in range(cases):
         send_faces(0, c)
+    widen_start(0)
 
     y_id = lax.broadcasted_iota(jnp.int32, (rows, lanes), 0)
     z_id = lax.broadcasted_iota(jnp.int32, (rows, lanes), 1)
@@ -168,37 +197,39 @@
     def prev_z(value):
         return pltpu.roll(value, 1, value.ndim - 1)
 
-    def cube_of(j):
-        value = d[j]
-        cube[j] = value * value * value
-
     total_planes = planes * n_space
 
-    def inv_of(j):
-        g = s * planes + j - 1
+    def cube_of(j, n=1):
+        value = d[pl.ds(j, n)]
+        cube[pl.ds(j, n)] = value * value * value
+
+    def inv_of(j, n=1):
+        g = s * planes + j - 1 + lax.broadcasted_iota(jnp.int32, (n, rows, lanes), 0)
         x_count = (g > 0).astype(F32) + (g < total_planes - 1).astype(F32)
-        inside = jnp.logical_and(g >= 0, g < total_planes).astype(F32)
-        value = jnp.where(d[j] > 0, d[j], 1.0)
-        inv[j] = inside / (value * (yz_count + x_count))
-
-    def coefficients(j):
-        here = cube[j]
-        face_lo = STIFF_MIN + 0.5 * (cube[j - 1] + here)
-        face_hi = STIFF_MIN + 0.5 * (here + cube[j + 1])
-        kx[j - 1] = face_lo
-        kx[j] = face_hi
+        inside = jnp.logical_and(g >= 0, g < total_planes)
+        value = jnp.where(inside, d[pl.ds(j, n)], 1.0)
+        inv[pl.ds(j, n)] = jnp.where(inside, 1.0 / (value * (yz_count + x_count)), 0.0)
+
+    def coefficients(j, n=1):
+        at = pl.ds(j - 1, n)
+        here = cube[pl.ds(j, n)]
+        face_lo = STIFF_MIN + 0.5 * (cube[at] + here)
+        face_hi = STIFF_MIN + 0.5 * (here + cube[pl.ds(j + 1, n)])
         y_hi = STIFF_MIN + 0.5 * (here + jnp.where(y_last, 0.0, next_y(here)))
         y_lo = STIFF_MIN + 0.5 * (here + jnp.where(y_first, 0.0, prev_y(here)))
         z_hi = STIFF_MIN + 0.5 * (here + jnp.where(z_last, 0.0, next_z(here)))
         z_lo = STIFF_MIN + 0.5 * (here + jnp.where(z_first, 0.0, prev_z(here)))
+        kept = (1 - sup_v[at]).astype(F32)
         diagonal = DIAG_SHIFT + face_hi + face_lo + y_hi + y_lo + z_hi + z_lo
-        kyp[j - 1] = jnp.where(y_last, 0.0, y_hi)
-        kym[j - 1] = jnp.where(y_first, 0.0, y_lo)
-        kzp[j - 1] = jnp.where(z_last, 0.0, z_hi)
-        kzm[j - 1] = jnp.where(z_first, 0.0, z_lo)
-        kept = (1 - sup_v[j - 1]).astype(F32)
-        keep[j - 1] = kept
-        rdk[j - 1] = kept / diagonal
+        scaled = kept / diagonal
+        kx[at] = face_lo
+        kx[pl.ds(j, n)] = face_hi
+        kyp[at] = jnp.where(y_last, 0.0, y_hi)
+        kym[at] = jnp.where(y_first, 0.0, y_lo)
+        kzp[at] = jnp.where(z_last, 0.0, z_hi)
+        kzm[at] = jnp.where(z_first, 0.0, z_lo)
+        keep[at] = kept
+        rdk[at] = scaled
 
     def around(value):
         return (
@@ -206,10 +237,10 @@
             + jnp.where(z_last, 0.0, next_z(value)) + jnp.where(z_first, 0.0, prev_z(value))
         )
 
-    def filter_sum(j):
-        here = inv[j]
-        total = 2.0 * here + inv[j - 1] + inv[j + 1] + around(here)
-        hsum[j - 1] = 1.5 * cube[j] * total
+    def filter_sum(j, n=1):
+        here = inv[pl.ds(j, n)]
+        total = 2.0 * here + inv[pl.ds(j - 1, n)] + inv[pl.ds(j + 1, n)] + around(here)
+        hsum[pl.ds(j - 1, n)] = 1.5 * cube[pl.ds(j, n)] * total
 
     def loop(start, stop, fn, unroll=1):
         def step(i, carry):
@@ -218,41 +249,51 @@
 
         lax.fori_loop(start, stop, step, 0, unroll=unroll)
 
+    def blocks(start, stop, size):
+        return [(j, min(size, stop - j)) for j in range(start, stop, size)]
+
+    inner = blocks(2, planes, 2)
+
     for copy in dens_loads:
         copy.wait()
-    loop(1, last, cube_of)
-    loop(1, last, inv_of)
-    loop(2, planes, coefficients)
-
-    def sweep(src, dst, c, j, factor):
-        centre = src[c, :, j]
-        load = f[c, :, j - 1]
-        total = load + kx[j - 1] * src[c, :, j - 1] + kx[j] * src[c, :, j + 1]
-        total = total + kyp[j - 1] * next_y(centre) + kym[j - 1] * prev_y(centre)
-        total = total + kzp[j - 1] * next_z(centre) + kzm[j - 1] * prev_z(centre)
-        result = (keep[j - 1] * (1.0 - factor)) * centre + (rdk[j - 1] * factor) * total
-        dst[c, :, j] = result
-        return load, result
-
-    def energy(c, j):
-        centre = s2[c, :, j]
-        low = centre - s2[c, :, j - 1]
-        high = centre - s2[c, :, j + 1]
+    for j, n in blocks(1, last, 2):
+        cube_of(j, n)
+    for j, n in inner:
+        coefficients(j, n)
+
+    def sweep(src, dst, c, j, n, factor):
+        at = pl.ds(j - 1, n)
+        centre = src[c, :, pl.ds(j, n)]
+        load = f[c, :, at]
+        total = load + kx[at] * src[c, :, at] + kx[pl.ds(j, n)] * src[c, :, pl.ds(j + 1, n)]
+        total = total + kyp[at] * next_y(centre) + kym[at] * prev_y(centre)
+        total = total + kzp[at] * next_z(centre) + kzm[at] * prev_z(centre)
+        result = (keep[at] * (1.0 - factor)) * centre + (rdk[at] * factor) * total
+        dst[c, :, pl.ds(j, n)] = result
+        return jnp.sum(jnp.sum(load * result, axis=0), axis=0)
+
+    def energy(c, j, n):
+        centre = s2[c, :, pl.ds(j, n)]
+        low = centre - s2[c, :, pl.ds(j - 1, n)]
+        high = centre - s2[c, :, pl.ds(j + 1, n)]
         y_hi = centre - jnp.where(y_last, 0.0, next_y(centre))
         y_lo = centre - jnp.where(y_first, 0.0, prev_y(centre))
         z_hi = centre - jnp.where(z_last, 0.0, next_z(centre))
         z_lo = centre - jnp.where(z_first, 0.0, prev_z(centre))
         squares = low * low + high * high + y_hi * y_hi + y_lo * y_lo + z_hi * z_hi + z_lo * z_lo
         value = jnp.sum(squares, axis=0)
-        e[c, j - 1] = value
-        return value * hsum[j - 1]
+        e[c, pl.ds(j - 1, n)] = value
+        return jnp.sum(value * hsum[pl.ds(j - 1, n)], axis=0)
 
     def interior_one(c):
         disp_load(c).wait()
         force_load(c).wait()
-        loop(2, planes, lambda j: sweep(v, s1, c, j, STEP_ONE), unroll=2)
+        for j, n in inner:
+            sweep(v, s1, c, j, n, STEP_ONE)
 
     loop(0, cases, interior_one)
+    widen_wait(0)
+    widen_start(1)
 
     @pl.when(has_lo)
     def _():
@@ -264,44 +305,36 @@
 
     cube_of(0)
     cube_of(last)
-    inv_of(0)
-    inv_of(last)
     coefficients(1)
     coefficients(planes)
-    loop(1, last, filter_sum)
-
-    zero = jnp.zeros((rows, lanes), F32)
-
-    def stage_one(c):
+
+    for c in range(cases):
         await_faces(0, c)
-        sweep(v, s1, c, 1, STEP_ONE)
-        sweep(v, s1, c, planes, STEP_ONE)
+        sweep(v, s1, c, 1, 1, STEP_ONE)
+        sweep(v, s1, c, planes, 1, STEP_ONE)
         send_faces(1, c)
 
-        def step(j, total):
-            load, result = sweep(s1, s2, c, j, STEP_TWO)
-            return total + jnp.sum(load * result, axis=0)
-
-        acc[0, c] = lax.fori_loop(2, planes, step, zero, unroll=2)
-
-    loop(0, cases, stage_one)
+    widen_wait(1)
+    widen_start(2)
+    for j, n in blocks(0, last + 1, 2):
+        inv_of(j, n)
+    for j, n in blocks(1, last, 2):
+        filter_sum(j, n)
+
+    def interior_two(c):
+        acc[0, c] = sum(sweep(s1, s2, c, j, n, STEP_TWO) for j, n in inner)
+
+    loop(0, cases, interior_two)
 
     def out_copy(c):
         return pltpu.make_async_copy(s2.at[c, :, own], out.at[c], out_sem.at[c])
 
-    def stage_two(c):
+    for c in range(cases):
         await_faces(1, c)
-        load, result = sweep(s1, s2, c, 1, STEP_TWO)
-        total = acc[0, c] + jnp.sum(load * result, axis=0)
-        load, result = sweep(s1, s2, c, planes, STEP_TWO)
-        acc[0, c] = total + jnp.sum(load * result, axis=0)
+        part = sweep(s1, s2, c, 1, 1, STEP_TWO)
+        acc[0, c] = acc[0, c] + part + sweep(s1, s2, c, planes, 1, STEP_TWO)
         send_faces(2, c)
         out_copy(c).start()
-        acc[1, c] = lax.fori_loop(
-            2, planes, lambda j, total: total + energy(c, j), zero, unroll=2
-        )
-
-    loop(0, cases, stage_two)
 
     lane = lax.broadcasted_iota(jnp.int32, (1, lanes), 1)
 
@@ -328,13 +361,21 @@
         pltpu.make_async_copy(whole(which), whole(which), grecv.at[which]).wait()
         return jnp.sum(gath[which], axis=0)
 
+    for k in range(2, len(distances)):
+        if k > 2:
+            widen_start(k)
+        widen_wait(k)
     gather_start(0)
 
-    def stage_three(c):
+    def interior_three(c):
+        acc[1, c] = sum(energy(c, j, n) for j, n in inner)
+
+    loop(0, cases, interior_three)
+
+    for c in range(cases):
         await_faces(2, c)
-        acc[1, c] = acc[1, c] + energy(c, 1) + energy(c, planes)
-
-    loop(0, cases, stage_three)
+        acc[1, c] = acc[1, c] + energy(c, 1, 1) + energy(c, planes, 1)
+
     gather_start(1)
 
     cells = total_planes * rows * lanes
@@ -350,16 +391,15 @@
         for c in range(cases)
     ]
 
-    def mix(j):
-        value = picks[0] * e[0, j - 1]
+    def mix(j, n=1):
+        at = pl.ds(j - 1, n)
+        value = picks[0] * e[0, at]
         for c in range(1, cases):
-            value = value + picks[c] * e[c, j - 1]
-        u[j] = value
+            value = value + picks[c] * e[c, at]
+        u[pl.ds(j, n)] = value
 
     mix(1)
     mix(planes)
-
-    other = 1 - mine if n_case == 2 else lax.rem(mine + 1, n_case)
 
     def rim(dst, index, peer, case, src):
         return pltpu.make_async_remote_copy(
@@ -381,7 +421,8 @@
         for copy in rims_down:
             copy.start()
 
-    loop(2, planes, mix, unroll=2)
+    for j, n in inner:
+        mix(j, n)
     across = rim(up.at[own], 4, s, other, own)
     across.start()
     across.wait_recv()
@@ -396,26 +437,24 @@
         for copy in rims_down:
             copy.wait_recv()
 
-    def product(j):
-        cube[j] = 1.5 * cube[j] * (u[j] + up[j])
-
-    loop(0, last + 1, product, unroll=2)
-
-    def filtered(j):
-        here = cube[j]
-        kx[j - 1] = inv[j] * (2.0 * here + cube[j - 1] + cube[j + 1] + around(here))
-
-    loop(1, last, filtered, unroll=2)
+    for j, n in blocks(0, last + 1, 2):
+        at = pl.ds(j, n)
+        cube[at] = 1.5 * cube[at] * (u[at] + up[at])
+
+    for j, n in blocks(1, last, 2):
+        here = cube[pl.ds(j, n)]
+        beside = cube[pl.ds(j - 1, n)] + cube[pl.ds(j + 1, n)]
+        kx[pl.ds(j - 1, n)] = inv[pl.ds(j, n)] * (2.0 * here + beside + around(here))
 
     sums = gather_wait(1)
     scale = jnp.sum(weights * jnp.where(valid, sums, 0.0), axis=1, keepdims=True) / cells + 1e-06
-
-    def update(j):
-        value = d[j] + MOVE_LIMIT * (kx[j - 1] / scale - 1.0)
+    gain = MOVE_LIMIT / scale
+
+    for j, n in blocks(1, last, 2):
+        at = pl.ds(j - 1, n)
+        value = d[pl.ds(j, n)] + (kx[at] * gain - MOVE_LIMIT)
         value = jnp.minimum(jnp.maximum(value, DENSITY_MIN), 1.0)
-        newd[j - 1] = jnp.where(void_v[j - 1] == 1, DENSITY_MIN, value)
-
-    loop(1, last, update, unroll=2)
+        newd[at] = jnp.where(void_v[at] == 1, DENSITY_MIN, value)
 
     @pl.when(has_hi)
     def _():
@@ -477,6 +516,7 @@
                 dma((2, cases)), dma((3,)), dma((cases,)),
                 dma((3, cases, 2)), dma((3, cases, 2)), dma((2,)), dma((2,)),
                 dma((5,)), dma((5,)), dma((2,)), dma((2,)),
+                pltpu.SemaphoreType.REGULAR((8,)),
             ],
             compiler_params=pltpu.CompilerParams(collective_id=0, has_side_effects=True),
         )(displacement, forces, density, support_mask, void_mask)

time: 34.2 us -> 32 us (0.936)
  Pallas kernels: 28.5 us -> 26.4 us
    pallas_call x1, Pallas kernels: 28.5 us -> 26.4 us  [body(): pl.pallas_call(functools.partial(kernel, n_space, n_case), out_shape=(jax...]
where the time goes in v2:
time: 32 us; the launch traced here: 31.8 us
  Pallas kernels  26.4 us (82%)
  local copies, waits for them, and re-layouts  3.04 us (10%)
  between operations  2.41 us (8%)
    pallas_call x1, Pallas kernels, body(): pl.pallas_call(functools.partial(kernel, n_space, n_case), out_shape=(jax...  26.4 us
    unnamed x4, local copies, waits for them, and re-layouts  3.04 us

profile of v2, /device:TPU:0, one launch (start us, length us, event | category | flops | bytes accessed | tf_op | source)
XLA Modules:
  0.0 31.8 jit_solution(11376121815299885239)
XLA Ops:
  0.6 26.4 %shard_map.76 = (f32[4,3,12,16,128]{4,3,2,1,0:T(8,128)}, f32[12,16,128]{2,1,0:T(8,128)}, f32[1]{0:T(128)}) custom-call(f32[4,3,12,16,128]{4,3,2,1,0:T(8,128)} %disp.1, f32[4,3,12,16,128]{4,3,2,1,0:T(8,128)} %forces.1, f32[12,16,128]{2,1,0:T(8,128)} %dens.1, s32[12,16,128]{2,1,0:T(8,128)} %sup.1, s32[12,16,128]{2,1,0:T(8,128)} %void.1), custom_call_target="tpu_custom_call" | custom-call | tf_op jit(solution)/shard_map/pallas_call | solution.py:493
  27.0 0.0 copy-start
  27.0 2.4 %copy.11 = f32[4,3,12,16,128]{4,3,2,1,0:T(8,128)} copy(f32[4,3,12,16,128]{4,3,2,1,0:T(8,128)} %get-tuple-element.6) | data formatting | bytes 2359296
  29.4 0.0 copy-done
  29.4 0.6 %copy.12 = f32[12,16,128]{2,1,0:T(8,128)} copy(f32[12,16,128]{2,1,0:T(8,128)S(1)} %copy-done) | data formatting | bytes 196608
Async XLA Ops:
  27.0 2.4 %copy-start = (f32[12,16,128]{2,1,0:T(8,128)S(1)}, f32[12,16,128]{2,1,0:T(8,128)}, u32[]{:S(2)}) copy-start(f32[12,16,128]{2,1,0:T(8,128)} %get-tuple-element.7) | copy-start | bytes 294916
